TPU v7x, 512 devices: a whole 4x8x8 slice. The times are simulated.
512 devices in a mesh: dp: 16 (over y, core), table: 32 (over x, z).
Axes of the slice: x: 4, y: 8, z: 8, core: 2. Of those that a mesh axis runs over, the one named last changes fastest.
Arguments:
- embedded: bfloat16 [2, 32768, 4096], P(None, 'dp', 'table'), may hold values from -1.1953125 to 1.1953125
- resid_grad: bfloat16 [2, 32768, 4096], P(None, 'dp', 'table'), may hold values from -0.29882812 to 0.29882812
- query_grad: bfloat16 [2, 32768, 2048], P(None, ('dp', 'table')), may hold values from -0.59765625 to 0.59765625
- query_weight: bfloat16 [4096, 2048], P('table'), may hold values from -0.09375 to 0.09375
- ngram_rows: int32 [2, 32768, 4], P(None, 'dp'), may hold values from 0 to 3199999, as said below
- touched_rows: int32 [32, 4, 12], replicated, may hold values from -1 to 3199999, as said below
- row_values: float32 [32, 4, 12, 1024], P('table'), may hold values from -6 to 6
- row_mean: float32 [32, 4, 12, 1024], P('table'), may hold values from -0.6 to 0.6
- row_square: float32 [32, 4, 12, 1024], P('table'), may hold values from 0.01 to 0.1
Outputs:
- weight_grad: float32 [4096, 2048], P('table')
- new_values: float32 [32, 4, 12, 1024], P('table')
- new_mean: float32 [32, 4, 12, 1024], P('table')
- new_square: float32 [32, 4, 12, 1024], P('table')
Inputs may be any that keep to these rules, and one draw needn't show every extreme that they name: `touched_rows`: owner o's list for slice s holds 1 to 12 distinct row ids of [o * 100000, (o + 1) * 100000) first, then -1; in every slice some owner's list is full. `ngram_rows`: every id of slice s is one of the listed rows of owner id // 100000 for slice s.
All inputs are finite; a program needn't handle non-finite values.
Results may differ from a plain program's by a relative error of at most 0.0003.
Values may be sent and summed in bfloat16 or wider, within the bound.
No kernel may reach another device: no remote copies, remote signals or barrier semaphores. Data moves between devices by JAX's collectives and lax.ppermute only.
A program may use at most 64 MiB of HBM per device.

v0:
```python
import jax
import jax.numpy as jnp
from jax import lax
from jax.sharding import PartitionSpec as P

SLICES = 4
SW = 1024
beta_one = 0.9
beta_two = 0.95
learn_rate = 0.01
adam_eps = 1e-08
adam_step = 10


def adam_rows(grads, values, mean, square, live):
    corr_one = 1.0 - beta_one**adam_step
    corr_two = 1.0 - beta_two**adam_step
    mean_next = beta_one * mean + (1.0 - beta_one) * grads
    square_next = beta_two * square + (1.0 - beta_two) * grads * grads
    update = learn_rate * (mean_next / corr_one) / (jnp.sqrt(square_next / corr_two) + adam_eps)
    values_next = values - update
    return (
        jnp.where(live, values_next, values),
        jnp.where(live, mean_next, mean),
        jnp.where(live, square_next, square),
    )


def make_step(emb_part, weight_part, carry, piece):
    back_part, wgrad = carry
    back = jnp.einsum("mrh,ph->mrp", piece, weight_part, preferred_element_type=jnp.float32)
    back_part = back
    wgrad = wgrad + jnp.einsum("mrp,mrh->ph", emb_part, piece, preferred_element_type=jnp.float32)
    return (back_part, wgrad)


def local(
    embedded,
    resid_grad,
    query_grad,
    query_weight,
    ngram_rows,
    touched_rows,
    row_values,
    row_mean,
    row_square,
):
    micro_count, group_tokens, width_part = embedded.shape
    hidden = query_grad.shape[2]
    tables = lax.axis_size("table")
    table_idx = lax.axis_index("table")
    zero_grad = jnp.zeros((width_part, hidden), jnp.float32)
    wgrad = zero_grad
    backs = []
    for micro in range(micro_count):
        start_back = jnp.zeros((1, group_tokens, width_part), jnp.float32)
        back_one, wgrad = make_step(
            embedded[micro : micro + 1],
            query_weight,
            (start_back, wgrad),
            lax.all_gather(query_grad[micro : micro + 1], "table", axis=1, tiled=True),
        )
        backs.append(back_one)
    back_all = jnp.concatenate(backs, axis=0)
    emb_grad = resid_grad.astype(jnp.float32) + back_all
    weight_grad = lax.psum(wgrad, "dp")
    slice_idx = table_idx * width_part // SW
    ids = lax.dynamic_index_in_dim(ngram_rows, slice_idx, 2, False)
    listed = lax.dynamic_index_in_dim(touched_rows, slice_idx, 1, False)
    entries = listed.shape[1]
    flat_list = listed.reshape(tables * entries)
    onehot = (ids[:, :, None] == flat_list[None, None, :]).astype(jnp.float32)
    buckets = jnp.einsum(
        "mtk,mtp->kp",
        onehot,
        emb_grad,
        precision=lax.Precision.HIGHEST,
        preferred_element_type=jnp.float32,
    )
    buckets = buckets.reshape(tables, entries, width_part)
    arrived = lax.all_to_all(buckets, "table", split_axis=0, concat_axis=0, tiled=True)
    per_slice = tables // SLICES
    local_grad = (
        arrived.reshape(SLICES, per_slice, entries, width_part)
        .transpose(0, 2, 1, 3)
        .reshape(SLICES, entries, per_slice * width_part)
    )
    mine = lax.dynamic_index_in_dim(touched_rows, table_idx, 0, False)
    live = (mine >= 0)[..., None]
    values = row_values[0]
    mean = row_mean[0]
    square = row_square[0]
    grads = lax.psum(local_grad, "dp")
    values_next, mean_next, square_next = adam_rows(grads, values, mean, square, live)
    return (weight_grad, values_next[None], mean_next[None], square_next[None])


def solution(mesh):
    placed = (
        P(None, "dp", "table"),
        P(None, "dp", "table"),
        P(None, ("dp", "table"), None),
        P("table", None),
        P(None, "dp", None),
        P(),
        P("table", None, None, None),
        P("table", None, None, None),
        P("table", None, None, None),
    )
    return jax.shard_map(
        local,
        mesh=mesh,
        in_specs=placed,
        out_specs=(
            P("table", None),
            P("table", None, None, None),
            P("table", None, None, None),
            P("table", None, None, None),
        ),
        check_vma=False,
    )
```

profile of v0, /device:TPU:25, one launch (start us, length us, event | category | flops | bytes accessed | tf_op | source)
XLA Modules:
  0.0 381.5 jit_solution(2230396503521548309)
XLA Ops:
  7.2 0.0 copy-start
  7.2 0.0 all-gather.5.cloned.1.call-start
  7.2 1.9 fusion.37
  9.1 0.0 all-gather.5.cloned.1.call-update
  9.2 0.0 all-gather.3.cloned.1.call-start
  9.2 0.7 all-gather.3.cloned.1.call-update
  9.9 0.9 constant_dynamic-slice_fusion.1
  10.8 0.8 constant_dynamic-slice_fusion
  11.6 0.1 copy.22
  11.7 0.1 eq.19
  11.8 107.7 %all-gather.5.cloned.1.call-done = bf16[1,2048,2048]{2,1,0:T(8,128)(2,1)} async-done(((bf16[1,64,2048]{2,1,0:T(8,128)(2,1)}), bf16[1,2048,2048]{2,1,0:T(8,128)(2,1)}) %all-gather.5.cloned.1.call-update) | async-done | bytes 8388624 | tf_op jit(solution)/shard_map/all_gather | solution.py:61
  119.5 0.0 copy-done
  119.5 6.7 %fusion.15 = f32[1,2048,128]{2,1,0:T(8,128)} fusion(bf16[128,2048]{1,0:T(8,128)(2,1)S(1)} %copy-done, bf16[1,2048,2048]{2,1,0:T(8,128)(2,1)} %all-gather.5.cloned.1.call-done), kind=kOutput, calls=%fused_computation.13 | convolution fusion | flops 1073741824 | bytes 9961472 | tf_op jit(solution)/shard_map/mrh,ph->mrp/dot_general | solution.py:31
  126.2 0.0 copy-start.6
  126.2 0.0 copy-start.1
  126.2 97.1 %all-gather.3.cloned.1.call-done = bf16[1,2048,2048]{2,1,0:T(8,128)(2,1)} async-done(((bf16[1,64,2048]{2,1,0:T(8,128)(2,1)}), bf16[1,2048,2048]{2,1,0:T(8,128)(2,1)}) %all-gather.3.cloned.1.call-update) | async-done | bytes 8388624 | tf_op jit(solution)/shard_map/all_gather | solution.py:61
  223.3 0.0 copy-start.7
  223.3 5.9 %fusion.12 = f32[1,2048,128]{2,1,0:T(8,128)S(1)} fusion(bf16[128,2048]{1,0:T(8,128)(2,1)S(1)} %copy-done, bf16[1,2048,2048]{2,1,0:T(8,128)(2,1)} %all-gather.3.cloned.1.call-done), kind=kOutput, calls=%fused_computation.12 | convolution fusion | flops 1073741824 | bytes 9961472 | tf_op jit(solution)/shard_map/mrh,ph->mrp/dot_general | solution.py:31
  229.1 0.0 copy-done.6
  229.1 0.0 copy-done.7
  229.2 3.1 fusion.24
  232.3 0.7 reshape.46
  233.0 5.2 %all-to-all-start = ((f32[32,12,128]{2,1,0:T(8,128)}), f32[32,12,128]{2,1,0:T(8,128)S(1)}, u32[]{:S(2)}, u32[]{:S(2)}) async-start(f32[32,12,128]{2,1,0:T(8,128)} %reshape.46), calls=%async_computation | async-start | bytes 524288 | tf_op jit(solution)/shard_map/all_to_all | solution.py:81
  238.1 0.2 all-reduce.3.cloned.1.call-start
  238.4 0.0 copy-done.1
  238.4 4.7 %fusion.2 = f32[128,2048]{1,0:T(8,128)S(1)} fusion(bf16[1,2048,2048]{2,1,0:T(8,128)(2,1)} %all-gather.5.cloned.1.call-done, bf16[2,2048,128]{2,1,0:T(8,128)(2,1)S(1)} %copy-done.1), kind=kOutput, calls=%fused_computation.2 | convolution fusion | flops 1073741824 | bytes 9961472 | tf_op jit(solution)/shard_map/mrp,mrh->ph/dot_general | solution.py:33
  243.0 0.0 copy-start.5
  243.1 0.0 copy-start.2
  243.1 0.0 copy-start.3
  243.1 0.0 copy-start.4
  243.1 5.7 %fusion.18 = f32[128,2048]{1,0:T(8,128)} fusion(f32[128,2048]{1,0:T(8,128)S(1)} %fusion.2, bf16[1,2048,2048]{2,1,0:T(8,128)(2,1)} %all-gather.3.cloned.1.call-done, bf16[2,2048,128]{2,1,0:T(8,128)(2,1)S(1)} %copy-done.1), kind=kOutput, calls=%fused_computation.14 | convolution fusion | flops 1074003968 | bytes 11010048 | tf_op jit(solution)/shard_map/mrp,mrh->ph/dot_general | solution.py:33
  248.8 0.0 all-to-all-done
  248.8 0.1 copy.23
  248.9 0.7 reshape.48
  249.6 0.0 all-reduce.3.cloned.1.call-update
  249.6 0.0 copy-done.5
  249.6 0.1 constant_dynamic-slice_fusion.2
  249.7 0.1 copy.25
  249.8 0.1 copy.21
  250.0 120.6 %all-reduce.3.cloned.1.call-done = (f32[128,2048]{1,0:T(8,128)}, f32[4,12,1024]{2,0,1:T(4,128)}) async-done(((f32[128,2048]{1,0:T(8,128)}, f32[4,12,1024]{2,0,1:T(4,128)}), (f32[128,2048]{1,0:T(8,128)}, f32[4,12,1024]{2,0,1:T(4,128)})) %all-reduce.3.cloned.1.call-update) | async-done | bytes 1245200 | tf_op jit(solution)/shard_map/psum | solution.py:66
  370.5 0.0 copy-done.2
  370.5 0.0 copy-done.3
  370.5 0.0 copy-done.4
  370.6 2.1 fusion.33
  372.7 2.3 copy.30
  (2 shorter events, 0.0 us)
Async XLA Ops:
  7.2 112.3 %copy-start = (bf16[128,2048]{1,0:T(8,128)(2,1)S(1)}, bf16[128,2048]{1,0:T(8,128)(2,1)}, u32[]{:S(2)}) copy-start(bf16[128,2048]{1,0:T(8,128)(2,1)} %param.12) | copy-start | bytes 1572868
  7.2 112.3 %all-gather.5.cloned.1.call-start = ((), (), s32[]{:S(2)}) async-start(), calls=%async_computation.2 | async-start | bytes 8650752 | tf_op jit(solution)/shard_map/all_gather | solution.py:61
  9.2 214.1 %all-gather.3.cloned.1.call-start = ((), (), s32[]{:S(2)}) async-start(), calls=%async_computation.1 | async-start | bytes 8650752 | tf_op jit(solution)/shard_map/all_gather | solution.py:61
  126.2 103.0 %copy-start.6 = (bf16[2,2048,128]{2,1,0:T(8,128)(2,1)S(1)}, bf16[2,2048,128]{2,1,0:T(8,128)(2,1)}, u32[]{:S(2)}) copy-start(bf16[2,2048,128]{2,1,0:T(8,128)(2,1)} %param.10) | copy-start | bytes 3145732
  126.2 112.2 %copy-start.1 = (bf16[2,2048,128]{2,1,0:T(8,128)(2,1)S(1)}, bf16[2,2048,128]{2,1,0:T(8,128)(2,1)}, u32[]{:S(2)}) copy-start(bf16[2,2048,128]{2,1,0:T(8,128)(2,1)} %param.9) | copy-start | bytes 3145732
  223.3 5.9 %copy-start.7 = (f32[1,2048,128]{2,1,0:T(8,128)S(1)}, f32[1,2048,128]{2,1,0:T(8,128)}, u32[]{:S(2)}) copy-start(f32[1,2048,128]{2,1,0:T(8,128)} %fusion.15) | copy-start | bytes 3145732
  233.0 15.8 %all-to-all-start = ((f32[32,12,128]{2,1,0:T(8,128)}), f32[32,12,128]{2,1,0:T(8,128)S(1)}, u32[]{:S(2)}, u32[]{:S(2)}) async-start(f32[32,12,128]{2,1,0:T(8,128)} %reshape.46), calls=%async_computation | async-start | bytes 524288 | tf_op jit(solution)/shard_map/all_to_all | solution.py:81
  238.1 132.4 %all-reduce.3.cloned.1.call-start = ((), (), s32[]{:S(2)}) async-start(), calls=%async_computation.3 | async-start | bytes 2490368 | tf_op jit(solution)/shard_map/psum | solution.py:66
  243.0 6.6 %copy-start.5 = (s32[32,4,12]{0,1,2:T(4,128)S(1)}, s32[32,4,12]{0,1,2:T(4,128)}, u32[]{:S(2)}) copy-start(s32[32,4,12]{0,1,2:T(4,128)} %param.14) | copy-start | bytes 18436
  243.1 127.5 %copy-start.2 = (f32[1,4,12,1024]{3,1,2,0:T(4,128)S(1)}, f32[1,4,12,1024]{3,1,2,0:T(4,128)}, u32[]{:S(2)}) copy-start(f32[1,4,12,1024]{3,1,2,0:T(4,128)} %param.17) | copy-start | bytes 589828
  243.1 127.5 %copy-start.3 = (f32[1,4,12,1024]{3,1,2,0:T(4,128)S(1)}, f32[1,4,12,1024]{3,1,2,0:T(4,128)}, u32[]{:S(2)}) copy-start(f32[1,4,12,1024]{3,1,2,0:T(4,128)} %param.16) | copy-start | bytes 589828
  243.1 127.5 %copy-start.4 = (f32[1,4,12,1024]{3,1,2,0:T(4,128)S(1)}, f32[1,4,12,1024]{3,1,2,0:T(4,128)}, u32[]{:S(2)}) copy-start(f32[1,4,12,1024]{3,1,2,0:T(4,128)} %param.15) | copy-start | bytes 589828
Sparse Core Ops, SparseCore 0:
  11.7 107.6 all-gather.4
  122.6 100.5 all-gather.2
  249.8 120.7 all-reduce.2
where the time goes:
time: 382 us
  waiting for transfers between devices  326 us (85%)
  matrix products  26 us (7%)
  between operations  13.9 us (4%)
  local copies, waits for them, and re-layouts  7.9 us (2%)
  starting transfers between devices  5.46 us (1%)
    all_gather x2, waiting for transfers between devices, local(): lax.all_gather(query_grad[micro:micro + 1], 'table', axis=1, tiled=True)  205 us
    psum x1, waiting for transfers between devices, local(): weight_grad = lax.psum(wgrad, 'dp')  121 us
    dot_general x2, matrix products, make_step(): jnp.einsum('mrh,ph->mrp', piece, weight_part, preferred_element_type=jnp....  12.6 us
    dot_general x2, matrix products, make_step(): jnp.einsum('mrp,mrh->ph', emb_part, piece, preferred_element_type=jnp.flo...  10.4 us
  transfers between devices with their start and end apart: 4, of which 3 were waited for; matrix products, arithmetic and copies ran while one was open for 5% of the time, Pallas kernels for 0%

commit v1 on v0

--- a/solution.py
+++ b/solution.py
@@ -63,7 +63,7 @@
         backs.append(back_one)
     back_all = jnp.concatenate(backs, axis=0)
     emb_grad = resid_grad.astype(jnp.float32) + back_all
-    weight_grad = lax.psum(wgrad, "dp")
+    weight_grad = jnp.sum(lax.all_gather(wgrad, "dp"), axis=0)
     slice_idx = table_idx * width_part // SW
     ids = lax.dynamic_index_in_dim(ngram_rows, slice_idx, 2, False)
     listed = lax.dynamic_index_in_dim(touched_rows, slice_idx, 1, False)

time: 382 us -> 476 us (1.25)
  the two profiles are of different devices: /device:TPU:25 before, /device:TPU:1 now
where the time goes in v1:
time: 476 us
  waiting for transfers between devices  414 us (87%)
  matrix products  26 us (5%)
  between operations  13.9 us (3%)
  other arithmetic  10.6 us (2%)
  local copies, waits for them, and re-layouts  5.6 us (1%)
  starting transfers between devices  5.51 us (1%)
    all_gather x2, waiting for transfers between devices, local(): lax.all_gather(query_grad[micro:micro + 1], 'table', axis=1, tiled=True)  206 us
    psum x1, waiting for transfers between devices, local(): grads = lax.psum(local_grad, 'dp')  104 us
    all_gather x1, waiting for transfers between devices, local(): weight_grad = jnp.sum(lax.all_gather(wgrad, 'dp'), axis=0)  98.7 us
    dot_general x2, matrix products, make_step(): jnp.einsum('mrh,ph->mrp', piece, weight_part, preferred_element_type=jnp....  12.6 us
    dot_general x2, matrix products, make_step(): jnp.einsum('mrp,mrh->ph', emb_part, piece, preferred_element_type=jnp.flo...  10.3 us
  transfers between devices with their start and end apart: 5, of which 5 were waited for; matrix products, arithmetic and copies ran while one was open for 4% of the time, Pallas kernels for 0%

profile of v1, /device:TPU:1, one launch (start us, length us, event | category | flops | bytes accessed | tf_op | source)
XLA Modules:
  0.0 475.8 jit_solution(15537818647815510272)
XLA Ops:
  7.2 0.0 copy-start
  7.2 0.0 all-gather.7.cloned.1.call-start
  7.2 1.9 fusion.37
  9.1 0.0 all-gather.7.cloned.1.call-update
  9.2 0.0 all-gather.5.cloned.1.call-start
  9.2 0.7 all-gather.5.cloned.1.call-update
  9.9 0.8 constant_dynamic-slice_fusion
  10.7 0.1 copy.22
  10.8 0.1 eq.19
  10.9 0.9 constant_dynamic-slice_fusion.1
  11.8 108.8 %all-gather.7.cloned.1.call-done = bf16[1,2048,2048]{2,1,0:T(8,128)(2,1)} async-done(((bf16[1,64,2048]{2,1,0:T(8,128)(2,1)}), bf16[1,2048,2048]{2,1,0:T(8,128)(2,1)}) %all-gather.7.cloned.1.call-update) | async-done | bytes 8388624 | tf_op jit(solution)/shard_map/all_gather | solution.py:61
  120.6 0.0 copy-done
  120.6 6.7 %fusion.15 = f32[1,2048,128]{2,1,0:T(8,128)} fusion(bf16[128,2048]{1,0:T(8,128)(2,1)S(1)} %copy-done, bf16[1,2048,2048]{2,1,0:T(8,128)(2,1)} %all-gather.7.cloned.1.call-done), kind=kOutput, calls=%fused_computation.13 | convolution fusion | flops 1073741824 | bytes 9961472 | tf_op jit(solution)/shard_map/mrh,ph->mrp/dot_general | solution.py:31
  127.3 0.0 copy-start.6
  127.3 0.0 copy-start.1
  127.3 97.1 %all-gather.5.cloned.1.call-done = bf16[1,2048,2048]{2,1,0:T(8,128)(2,1)} async-done(((bf16[1,64,2048]{2,1,0:T(8,128)(2,1)}), bf16[1,2048,2048]{2,1,0:T(8,128)(2,1)}) %all-gather.5.cloned.1.call-update) | async-done | bytes 8388624 | tf_op jit(solution)/shard_map/all_gather | solution.py:61
  224.4 0.0 copy-start.7
  224.4 5.8 %fusion.12 = f32[1,2048,128]{2,1,0:T(8,128)S(1)} fusion(bf16[128,2048]{1,0:T(8,128)(2,1)S(1)} %copy-done, bf16[1,2048,2048]{2,1,0:T(8,128)(2,1)} %all-gather.5.cloned.1.call-done), kind=kOutput, calls=%fused_computation.12 | convolution fusion | flops 1073741824 | bytes 9961472 | tf_op jit(solution)/shard_map/mrh,ph->mrp/dot_general | solution.py:31
  230.2 0.0 copy-done.6
  230.2 0.0 copy-done.7
  230.2 3.1 fusion.24
  233.3 0.7 reshape.46
  234.1 5.2 %all-to-all-start = ((f32[32,12,128]{2,1,0:T(8,128)}), f32[32,12,128]{2,1,0:T(8,128)S(1)}, u32[]{:S(2)}, u32[]{:S(2)}) async-start(f32[32,12,128]{2,1,0:T(8,128)} %reshape.46), calls=%async_computation | async-start | bytes 524288 | tf_op jit(solution)/shard_map/all_to_all | solution.py:81
  239.2 0.0 all-reduce.2.cloned.1.call-start
  239.3 0.0 copy-done.1
  239.3 4.7 fusion.2
  244.0 4.9 %all-to-all-done = f32[32,12,128]{2,1,0:T(8,128)S(1)} async-done(((f32[32,12,128]{2,1,0:T(8,128)}), f32[32,12,128]{2,1,0:T(8,128)S(1)}, u32[]{:S(2)}, u32[]{:S(2)}) %all-to-all-start) | async-done | bytes 196640 | tf_op jit(solution)/shard_map/all_to_all | solution.py:81
  248.9 0.1 copy.23
  249.0 0.7 reshape.48
  249.7 0.0 all-reduce.2.cloned.1.call-update
  249.7 0.0 copy-start.5
  249.7 0.0 copy-start.2
  249.7 0.0 copy-start.3
  249.8 0.0 copy-start.4
  249.8 0.2 all-gather.9.cloned.1.call-start
  250.0 5.7 %fusion.18 = f32[128,2048]{1,0:T(8,128)} fusion(f32[128,2048]{1,0:T(8,128)S(1)} %fusion.2, bf16[1,2048,2048]{2,1,0:T(8,128)(2,1)} %all-gather.5.cloned.1.call-done, bf16[2,2048,128]{2,1,0:T(8,128)(2,1)S(1)} %copy-done.1), kind=kOutput, calls=%fused_computation.14 | convolution fusion | flops 1074003968 | bytes 11010048 | tf_op jit(solution)/shard_map/mrp,mrh->ph/dot_general | solution.py:33
  255.7 0.0 all-gather.9.cloned.1.call-update
  255.7 0.0 copy-done.5
  255.7 0.1 constant_dynamic-slice_fusion.2
  255.8 0.1 copy.25
  255.9 0.1 copy.21
  256.0 104.0 %all-reduce.2.cloned.1.call-done = f32[4,12,1024]{2,0,1:T(4,128)} async-done(((f32[4,12,1024]{2,0,1:T(4,128)}), f32[4,12,1024]{2,0,1:T(4,128)}) %all-reduce.2.cloned.1.call-update) | async-done | bytes 196624 | tf_op jit(solution)/shard_map/psum | solution.py:93
  360.0 0.0 copy-done.2
  360.0 0.0 copy-done.3
  360.0 0.0 copy-done.4
  360.0 2.1 fusion.33
  362.2 98.7 %all-gather.9.cloned.1.call-done = f32[2048,2048]{1,0:T(8,128)} async-done(((f32[128,2048]{1,0:T(8,128)}), f32[2048,2048]{1,0:T(8,128)}) %all-gather.9.cloned.1.call-update) | async-done | bytes 16777232 | tf_op jit(solution)/shard_map/all_gather | solution.py:66
  460.8 8.4 %reduce_sum.9 = f32[128,2048]{1,0:T(8,128)} reduce(f32[16,128,2048]{2,1,0:T(8,128)} %bitcast.75, f32[]{:T(128)} %constant.22.clone.1), dimensions={0}, to_apply=%region_0.0 | reduce | flops 3932160 | bytes 17825796 | tf_op jit(solution)/shard_map/reduce_sum | solution.py:66
  (2 shorter events, 0.0 us)
Async XLA Ops:
  7.2 113.4 %copy-start = (bf16[128,2048]{1,0:T(8,128)(2,1)S(1)}, bf16[128,2048]{1,0:T(8,128)(2,1)}, u32[]{:S(2)}) copy-start(bf16[128,2048]{1,0:T(8,128)(2,1)} %param.12) | copy-start | bytes 1572868
  7.2 113.4 %all-gather.7.cloned.1.call-start = ((), (), s32[]{:S(2)}) async-start(), calls=%async_computation.2 | async-start | bytes 8650752 | tf_op jit(solution)/shard_map/all_gather | solution.py:61
  9.2 215.2 %all-gather.5.cloned.1.call-start = ((), (), s32[]{:S(2)}) async-start(), calls=%async_computation.1 | async-start | bytes 8650752 | tf_op jit(solution)/shard_map/all_gather | solution.py:61
  127.3 103.0 %copy-start.6 = (bf16[2,2048,128]{2,1,0:T(8,128)(2,1)S(1)}, bf16[2,2048,128]{2,1,0:T(8,128)(2,1)}, u32[]{:S(2)}) copy-start(bf16[2,2048,128]{2,1,0:T(8,128)(2,1)} %param.10) | copy-start | bytes 3145732
  127.3 112.0 %copy-start.1 = (bf16[2,2048,128]{2,1,0:T(8,128)(2,1)S(1)}, bf16[2,2048,128]{2,1,0:T(8,128)(2,1)}, u32[]{:S(2)}) copy-start(bf16[2,2048,128]{2,1,0:T(8,128)(2,1)} %param.9) | copy-start | bytes 3145732
  224.4 5.9 %copy-start.7 = (f32[1,2048,128]{2,1,0:T(8,128)S(1)}, f32[1,2048,128]{2,1,0:T(8,128)}, u32[]{:S(2)}) copy-start(f32[1,2048,128]{2,1,0:T(8,128)} %fusion.15) | copy-start | bytes 3145732
  234.1 14.8 %all-to-all-start = ((f32[32,12,128]{2,1,0:T(8,128)}), f32[32,12,128]{2,1,0:T(8,128)S(1)}, u32[]{:S(2)}, u32[]{:S(2)}) async-start(f32[32,12,128]{2,1,0:T(8,128)} %reshape.46), calls=%async_computation | async-start | bytes 524288 | tf_op jit(solution)/shard_map/all_to_all | solution.py:81
  239.2 120.8 %all-reduce.2.cloned.1.call-start = ((), (), s32[]{:S(2)}) async-start(), calls=%async_computation.3 | async-start | bytes 393216 | tf_op jit(solution)/shard_map/psum | solution.py:93
  249.7 6.0 %copy-start.5 = (s32[32,4,12]{0,1,2:T(4,128)S(1)}, s32[32,4,12]{0,1,2:T(4,128)}, u32[]{:S(2)}) copy-start(s32[32,4,12]{0,1,2:T(4,128)} %param.14) | copy-start | bytes 18436
  249.7 110.3 %copy-start.2 = (f32[1,4,12,1024]{3,1,2,0:T(4,128)S(1)}, f32[1,4,12,1024]{3,1,2,0:T(4,128)}, u32[]{:S(2)}) copy-start(f32[1,4,12,1024]{3,1,2,0:T(4,128)} %param.17) | copy-start | bytes 589828
  249.7 110.3 %copy-start.3 = (f32[1,4,12,1024]{3,1,2,0:T(4,128)S(1)}, f32[1,4,12,1024]{3,1,2,0:T(4,128)}, u32[]{:S(2)}) copy-start(f32[1,4,12,1024]{3,1,2,0:T(4,128)} %param.16) | copy-start | bytes 589828
  249.8 110.3 %copy-start.4 = (f32[1,4,12,1024]{3,1,2,0:T(4,128)S(1)}, f32[1,4,12,1024]{3,1,2,0:T(4,128)}, u32[]{:S(2)}) copy-start(f32[1,4,12,1024]{3,1,2,0:T(4,128)} %param.15) | copy-start | bytes 589828
  249.8 211.1 %all-gather.9.cloned.1.call-start = ((), (), s32[]{:S(2)}) async-start(), calls=%async_computation.4 | async-start | bytes 17825792 | tf_op jit(solution)/shard_map/all_gather | solution.py:66
Sparse Core Ops, SparseCore 0:
  11.7 108.7 all-gather.6
  123.7 100.5 all-gather.4
  249.8 110.1 all-reduce.1
  362.6 98.2 all-gather.8
